TPU v7x, 32 devices: a whole 2x2x4 slice. The times are simulated.
32 devices in a mesh: dp: 8 (over y, x, core), ffn: 4 (over z).
Axes of the slice: x: 2, y: 2, z: 4, core: 2. Of those that a mesh axis runs over, the one named last changes fastest.
Arguments:
- layer_activations: bfloat16 [64, 512, 768], P(('dp', 'ffn')), may hold values from -6 to 6
- token_counts_each: int32 [64], P(('dp', 'ffn')), may hold values from 64 to 512, as said below
- attention_triple_matrix: bfloat16 [768, 2304], P('dp', 'ffn'), may hold values from -0.21875 to 0.21875
- attention_final_matrix: bfloat16 [768, 768], P('dp', 'ffn'), may hold values from -1.75 to 1.75
- feedfwd_expand_matrix: bfloat16 [768, 3072], P('dp', 'ffn'), may hold values from -0.21875 to 0.21875
- feedfwd_expand_offset: bfloat16 [3072], P('ffn'), may hold values from -3 to 3
- feedfwd_contract_matrix: bfloat16 [3072, 768], P('ffn', 'dp'), may hold values from -0.109375 to 0.109375
- layernorm_scales: bfloat16 [2, 768], P(None, 'dp'), may hold values from 0.25 to 1.75
- offset_vectors: bfloat16 [6, 768], P(None, 'dp'), may hold values from -2 to 2
- learned_gate_scores: bfloat16 [512, 512], P('dp', 'ffn'), may hold values from -5 to 5
- fixed_jitter_matrix: bfloat16 [512, 512], P('dp', 'ffn'), may hold values from -1 to 1
- relaxation_heat: float32 [1], replicated, may hold values from 0.67 to 1
- loss_grad_result: bfloat16 [64, 512, 768], P(('dp', 'ffn')), may hold values from -6 to 6
Outputs:
- outputs: bfloat16 [64, 512, 768], P(('dp', 'ffn'))
- grad_inputs: float32 [64, 512, 768], P(('dp', 'ffn'))
- grad_w_qkv: float32 [768, 2304], P('dp', 'ffn')
- grad_w_out: float32 [768, 768], P('dp', 'ffn')
- grad_w_up: float32 [768, 3072], P('dp', 'ffn')
- grad_b_up: float32 [3072], P('ffn')
- grad_w_down: float32 [3072, 768], P('ffn', 'dp')
- grad_gains: float32 [2, 768], P(None, 'dp')
- grad_shifts: float32 [6, 768], P(None, 'dp')
- grad_logits: float32 [512, 512], P('dp', 'ffn')
Inputs may be any that keep to these rules, and one draw needn't show every extreme that they name: `token_counts_each`: number of real tokens of a sequence; the other positions of its 512 are padding, and only key positions are masked; some sequence has exactly 512 and some exactly 64.
All inputs are finite; a program needn't handle non-finite values.
Results may differ from a plain program's by a relative error of at most 0.012.
The roundings to bfloat16 on the way count: a program that leaves them out, or rounds other values in their place, can miss the bound.
Values may be sent and summed in bfloat16 or wider, within the bound.
A program may use at most 192 MiB of HBM per device.

v0:
```python
import jax
import jax.numpy as jnp
from jax import lax
from jax.sharding import PartitionSpec as P

D = 768
HEADS = 12
HEAD_DIM = 64
SEQ_LEN = 512
MICRO = 2
norm_eps = 1e-06


def split_up(value, dim, size):
    dims = value.shape
    parts = value.reshape(*dims[:dim], size, dims[dim] // size, *dims[dim + 1 :])
    return jnp.moveaxis(parts, dim, 0)


def summed_on_arrival(value, axis, dim):
    parts = split_up(value, dim, lax.axis_size(axis))
    arrived = lax.all_to_all(parts, axis, split_axis=0, concat_axis=0, tiled=True)
    return arrived.astype(jnp.float32).sum(axis=0)


def assemble(tile_stack, rows_dp, cols_ffn):
    count_all, first_len, second_len = tile_stack.shape
    grid = tile_stack.reshape(rows_dp, cols_ffn, first_len, second_len)
    return grid.transpose(0, 2, 1, 3).reshape(rows_dp * first_len, cols_ffn * second_len)


def disperse(full_grad, rows_dp, cols_ffn):
    total_rows, total_cols = full_grad.shape
    grid = full_grad.reshape(rows_dp, total_rows // rows_dp, cols_ffn, total_cols // cols_ffn)
    return grid.transpose(0, 2, 1, 3).reshape(
        rows_dp * cols_ffn, total_rows // rows_dp, total_cols // cols_ffn
    )


def vector_join(tile_stack, rows_dp, cols_ffn):
    count_all, kinds_count, part_len = tile_stack.shape
    picked = tile_stack.reshape(rows_dp, cols_ffn, kinds_count, part_len)[:, 0]
    return picked.transpose(1, 0, 2).reshape(kinds_count, rows_dp * part_len)


def vector_split(full_grad, rows_dp, cols_ffn):
    kinds_count, width_all = full_grad.shape
    part_len = width_all // rows_dp
    pieces = full_grad.reshape(kinds_count, rows_dp, part_len).transpose(1, 0, 2)
    spread = jnp.broadcast_to(pieces[:, None], (rows_dp, cols_ffn, kinds_count, part_len))
    return spread.reshape(rows_dp * cols_ffn, kinds_count, part_len)


def dot_first(left, right):
    return lax.dot_general(
        left, right, (((0,), (0,)), ((), ())), preferred_element_type=jnp.float32
    )


def dot_last(left, right):
    return lax.dot_general(
        left, right, (((1,), (1,)), ((), ())), preferred_element_type=jnp.float32
    )


def layer_norm(values, gain, shift):
    mean_row = jnp.mean(values, axis=-1, keepdims=True)
    centered = values - mean_row
    inv_std = lax.rsqrt(jnp.mean(centered * centered, axis=-1, keepdims=True) + norm_eps)
    normed = centered * inv_std
    return (normed * gain + shift, normed, inv_std)


def norm_back(grad_out, normed, inv_std, gain):
    grad_normed = grad_out * gain
    grad_in = inv_std * (
        grad_normed
        - jnp.mean(grad_normed, axis=-1, keepdims=True)
        - normed * jnp.mean(grad_normed * normed, axis=-1, keepdims=True)
    )
    return (grad_in, jnp.sum(grad_out * normed, axis=0), jnp.sum(grad_out, axis=0))


def gelu_slope(values):
    return (
        0.5 * (1.0 + lax.erf(values * 0.7071067811865476))
        + values * jnp.exp(-0.5 * values * values) * 0.3989422804014327
    )


def score_block(queries, keys_low, natural_log_gate, live):
    scores = (
        jnp.einsum("sqhd,skhd->shqk", queries, keys_low, preferred_element_type=jnp.float32)
        * HEAD_DIM ** (-0.5)
        + natural_log_gate
    )
    return jnp.where(live[:, None, None, :], scores, -1e30)


def attend(queries, keys_low, values_low, natural_log_gate, live):
    scores = score_block(queries, keys_low, natural_log_gate, live)
    peak = jnp.max(scores, axis=-1, keepdims=True)
    shifted_exp = jnp.exp(scores - peak)
    total_exp = jnp.sum(shifted_exp, axis=-1, keepdims=True)
    probs_low = (shifted_exp / total_exp).astype(jnp.bfloat16)
    context = jnp.einsum(
        "shqk,skhd->sqhd", probs_low, values_low, preferred_element_type=jnp.float32
    )
    return (context, peak + jnp.log(total_exp))


def attend_back(queries, keys_low, values_low, natural_log_gate, live, log_total, grad_context):
    scores = score_block(queries, keys_low, natural_log_gate, live)
    probs = jnp.exp(scores - log_total)
    grad_probs = jnp.einsum(
        "sqhd,skhd->shqk", grad_context, values_low, preferred_element_type=jnp.float32
    )
    grad_values = jnp.einsum(
        "shqk,sqhd->skhd",
        probs.astype(jnp.bfloat16),
        grad_context,
        preferred_element_type=jnp.float32,
    )
    grad_scores = probs * (grad_probs - jnp.sum(probs * grad_probs, axis=-1, keepdims=True))
    grad_mask = jnp.sum(grad_scores, axis=(0, 1))
    grad_scores_low = grad_scores.astype(jnp.bfloat16)
    grad_queries = jnp.einsum(
        "shqk,skhd->sqhd", grad_scores_low, keys_low, preferred_element_type=jnp.float32
    ) * HEAD_DIM ** (-0.5)
    grad_keys = jnp.einsum(
        "shqk,sqhd->skhd", grad_scores_low, queries, preferred_element_type=jnp.float32
    ) * HEAD_DIM ** (-0.5)
    return (grad_queries, grad_keys, grad_values, grad_mask)


def fetch_weights(
    attention_triple_matrix,
    attention_final_matrix,
    feedfwd_expand_matrix,
    feedfwd_contract_matrix,
    layernorm_scales,
    offset_vectors,
    learned_gate_scores,
    fixed_jitter_matrix,
    relaxation_heat,
):
    rows_dp = lax.axis_size("dp")
    cols_ffn = lax.axis_size("ffn")
    tiles = (
        lax.all_gather(attention_triple_matrix[None], ("dp", "ffn"), axis=0, tiled=True),
        lax.all_gather(attention_final_matrix[None], ("dp", "ffn"), axis=0, tiled=True),
        lax.all_gather(learned_gate_scores[None], ("dp", "ffn"), axis=0, tiled=True),
        lax.all_gather(fixed_jitter_matrix[None], ("dp", "ffn"), axis=0, tiled=True),
        lax.all_gather(layernorm_scales[None], ("dp", "ffn"), axis=0, tiled=True),
        lax.all_gather(offset_vectors[None], ("dp", "ffn"), axis=0, tiled=True),
    )
    ffn_parts = (
        lax.all_gather(feedfwd_expand_matrix, "dp", axis=0, tiled=True),
        lax.all_gather(feedfwd_contract_matrix, "dp", axis=1, tiled=True),
    )
    combined_attention_scores = (
        assemble(tiles[2], rows_dp, cols_ffn).astype(jnp.float32)
        + assemble(tiles[3], rows_dp, cols_ffn).astype(jnp.float32)
    ) / relaxation_heat[0]
    natural_log_gate = jax.nn.log_sigmoid(combined_attention_scores)
    gate_sharpness = jax.nn.sigmoid(-combined_attention_scores) / relaxation_heat[0]
    return (
        assemble(tiles[0], rows_dp, cols_ffn),
        assemble(tiles[1], rows_dp, cols_ffn),
        natural_log_gate,
        gate_sharpness,
        vector_join(tiles[4], rows_dp, cols_ffn).astype(jnp.float32),
        vector_join(tiles[5], rows_dp, cols_ffn).astype(jnp.float32),
        ffn_parts[0],
        ffn_parts[1],
    )


def reduce_grads(local_grads):
    rows_dp = lax.axis_size("dp")
    cols_ffn = lax.axis_size("ffn")
    grad_qkv, grad_out, grad_logit, grad_gain, grad_shift, grad_up, grad_down, grad_bias_up = (
        local_grads
    )
    attn_parts = (
        lax.psum_scatter(
            disperse(grad_qkv, rows_dp, cols_ffn), ("dp", "ffn"), scatter_dimension=0, tiled=True
        ),
        lax.psum_scatter(
            disperse(grad_out, rows_dp, cols_ffn), ("dp", "ffn"), scatter_dimension=0, tiled=True
        ),
        lax.psum_scatter(
            disperse(grad_logit, rows_dp, cols_ffn), ("dp", "ffn"), scatter_dimension=0, tiled=True
        ),
        lax.psum_scatter(
            vector_split(grad_gain, rows_dp, cols_ffn),
            ("dp", "ffn"),
            scatter_dimension=0,
            tiled=True,
        ),
        lax.psum_scatter(
            vector_split(grad_shift, rows_dp, cols_ffn),
            ("dp", "ffn"),
            scatter_dimension=0,
            tiled=True,
        ),
    )
    bias_rows = jnp.broadcast_to(grad_bias_up[None], (rows_dp, grad_bias_up.shape[0]))
    ffn_parts = (
        summed_on_arrival(grad_up.astype(jnp.bfloat16), "dp", 0),
        summed_on_arrival(grad_down.astype(jnp.bfloat16), "dp", 1),
        summed_on_arrival(bias_rows.astype(jnp.bfloat16), "dp", 0),
    )
    return (
        attn_parts[0][0],
        attn_parts[1][0],
        attn_parts[2][0],
        attn_parts[3][0],
        attn_parts[4][0],
        ffn_parts[0],
        ffn_parts[1],
        ffn_parts[2][0],
    )


def micro_step(fetched, inputs_block, lengths_block, cot_block, feedfwd_expand_offset):
    (
        full_qkv,
        full_out,
        natural_log_gate,
        gate_sharpness,
        gains_full,
        shifts_full,
        full_up,
        full_down,
    ) = fetched
    seq_count = inputs_block.shape[0]
    row_count = seq_count * SEQ_LEN
    flat_in = inputs_block.reshape(row_count, D)
    qkv_bias = jnp.concatenate([shifts_full[0], jnp.zeros((D,), jnp.float32), shifts_full[1]])
    proj_low = (jnp.dot(flat_in, full_qkv, preferred_element_type=jnp.float32) + qkv_bias).astype(
        jnp.bfloat16
    )
    head_shape = (seq_count, SEQ_LEN, HEADS, HEAD_DIM)
    queries = proj_low[:, :D].reshape(head_shape)
    keys_low = proj_low[:, D : 2 * D].reshape(head_shape)
    values_low = proj_low[:, 2 * D :].reshape(head_shape)
    live = lax.broadcasted_iota(jnp.int32, (seq_count, SEQ_LEN), 1) < lengths_block[:, None]
    context, log_total = attend(queries, keys_low, values_low, natural_log_gate, live)
    context_low = context.reshape(row_count, D).astype(jnp.bfloat16)
    first_sum = (
        flat_in.astype(jnp.float32)
        + jnp.dot(context_low, full_out, preferred_element_type=jnp.float32)
        + shifts_full[2]
    )
    hidden, normed_one, inv_one = layer_norm(first_sum, gains_full[0], shifts_full[4])
    hidden_low = hidden.astype(jnp.bfloat16)
    gathered = lax.all_gather(hidden_low, "ffn", axis=0, tiled=True)
    pre_act = jnp.dot(
        gathered, full_up, preferred_element_type=jnp.float32
    ) + feedfwd_expand_offset.astype(jnp.float32)
    act_low = jax.nn.gelu(pre_act, approximate=False).astype(jnp.bfloat16)
    partial_out = jnp.dot(act_low, full_down, preferred_element_type=jnp.float32)
    ffn_out = lax.psum_scatter(partial_out, "ffn", scatter_dimension=0, tiled=True)
    second_sum = hidden + ffn_out + shifts_full[3]
    result, normed_two, inv_two = layer_norm(second_sum, gains_full[1], shifts_full[5])
    cot_flat = cot_block.reshape(row_count, D).astype(jnp.float32)
    grad_second, grad_gain_two, grad_shift_two = norm_back(
        cot_flat, normed_two, inv_two, gains_full[1]
    )
    grad_second_low = grad_second.astype(jnp.bfloat16)
    grad_gathered = lax.all_gather(grad_second_low, "ffn", axis=0, tiled=True)
    grad_w_down = dot_first(act_low, grad_gathered)
    grad_act = dot_last(grad_gathered, full_down)
    grad_pre = (grad_act * gelu_slope(pre_act)).astype(jnp.bfloat16)
    grad_bias_up = jnp.sum(grad_pre, axis=0, dtype=jnp.float32)
    grad_w_up = dot_first(gathered, grad_pre)
    grad_hidden_part = dot_last(grad_pre, full_up)
    grad_hidden_ffn = lax.psum_scatter(grad_hidden_part, "ffn", scatter_dimension=0, tiled=True)
    grad_hidden = grad_second + grad_hidden_ffn
    grad_first, grad_gain_one, grad_shift_one = norm_back(
        grad_hidden, normed_one, inv_one, gains_full[0]
    )
    grad_first_low = grad_first.astype(jnp.bfloat16)
    grad_w_out = dot_first(context_low, grad_first_low)
    grad_context = dot_last(grad_first_low, full_out).astype(jnp.bfloat16).reshape(head_shape)
    grad_queries, grad_keys, grad_values, grad_mask = attend_back(
        queries, keys_low, values_low, natural_log_gate, live, log_total, grad_context
    )
    grad_projected = jnp.concatenate(
        [
            grad_queries.reshape(row_count, D).astype(jnp.bfloat16),
            grad_keys.reshape(row_count, D).astype(jnp.bfloat16),
            grad_values.reshape(row_count, D).astype(jnp.bfloat16),
        ],
        axis=1,
    )
    grad_w_qkv = dot_first(flat_in, grad_projected)
    grad_inputs = grad_first + dot_last(grad_projected, full_qkv)
    grad_query_bias = jnp.sum(grad_projected[:, :D], axis=0, dtype=jnp.float32)
    grad_value_bias = jnp.sum(grad_projected[:, 2 * D :], axis=0, dtype=jnp.float32)
    grad_shift_all = jnp.stack(
        [
            grad_query_bias,
            grad_value_bias,
            jnp.sum(grad_first, axis=0),
            jnp.sum(grad_second, axis=0),
            grad_shift_one,
            grad_shift_two,
        ]
    )
    grad_gain_all = jnp.stack([grad_gain_one, grad_gain_two])
    grad_logit = grad_mask * gate_sharpness
    local_grads = (
        grad_w_qkv,
        grad_w_out,
        grad_logit,
        grad_gain_all,
        grad_shift_all,
        grad_w_up,
        grad_w_down,
        grad_bias_up,
    )
    return (
        result.astype(jnp.bfloat16).reshape(seq_count, SEQ_LEN, D),
        grad_inputs.reshape(seq_count, SEQ_LEN, D),
        local_grads,
    )


def on_device(
    layer_activations,
    token_counts_each,
    attention_triple_matrix,
    attention_final_matrix,
    feedfwd_expand_matrix,
    feedfwd_expand_offset,
    feedfwd_contract_matrix,
    layernorm_scales,
    offset_vectors,
    learned_gate_scores,
    fixed_jitter_matrix,
    relaxation_heat,
    loss_grad_result,
):
    seq_block = layer_activations.shape[0] // MICRO
    result_list = []
    grad_list = []
    summed = None
    for micro_index in range(MICRO):
        fetched = fetch_weights(
            attention_triple_matrix,
            attention_final_matrix,
            feedfwd_expand_matrix,
            feedfwd_contract_matrix,
            layernorm_scales,
            offset_vectors,
            learned_gate_scores,
            fixed_jitter_matrix,
            relaxation_heat,
        )
        begin = micro_index * seq_block
        result_block, grad_block, local_grads = micro_step(
            fetched,
            layer_activations[begin : begin + seq_block],
            token_counts_each[begin : begin + seq_block],
            loss_grad_result[begin : begin + seq_block],
            feedfwd_expand_offset,
        )
        result_list.append(result_block)
        grad_list.append(grad_block)
        reduced = reduce_grads(local_grads)
        if summed is None:
            summed = reduced
        else:
            summed = tuple((left + right for left, right in zip(summed, reduced)))
    return (
        jnp.concatenate(result_list, axis=0),
        jnp.concatenate(grad_list, axis=0),
        summed[0],
        summed[1],
        summed[5],
        summed[7],
        summed[6],
        summed[3],
        summed[4],
        summed[2],
    )


def solution(mesh):
    in_specs = (
        P(("dp", "ffn"), None, None),
        P(("dp", "ffn")),
        P("dp", "ffn"),
        P("dp", "ffn"),
        P("dp", "ffn"),
        P("ffn"),
        P("ffn", "dp"),
        P(None, "dp"),
        P(None, "dp"),
        P("dp", "ffn"),
        P("dp", "ffn"),
        P(),
        P(("dp", "ffn"), None, None),
    )
    out_specs = (
        P(("dp", "ffn"), None, None),
        P(("dp", "ffn"), None, None),
        P("dp", "ffn"),
        P("dp", "ffn"),
        P("dp", "ffn"),
        P("ffn"),
        P("ffn", "dp"),
        P(None, "dp"),
        P(None, "dp"),
        P("dp", "ffn"),
    )
    return jax.shard_map(
        on_device, mesh=mesh, in_specs=in_specs, out_specs=out_specs, check_vma=False
    )
```

profile of v0, /device:TPU:0, one launch (start us, length us, event | category | flops | bytes accessed | tf_op | source)
XLA Modules:
  0.0 1699.8 jit_solution(4556506373768897747)
XLA Ops:
  13.2 69.5 %all-gather.7 = bf16[32,2,96]{2,1,0:T(2,128)(2,1)S(1)} all-gather(bf16[1,2,96]{2,1,0:T(2,128)(2,1)} %bitcast.336), channel_id=7, replica_groups=mesh['dp'=8,'ffn'=4] {'dp','ffn'}, dimensions={0}, use_global_device_ids=true | all-gather | bytes 12672 | tf_op jit(solution)/shard_map/all_gather | solution.py:154
  82.7 64.6 %all-gather.6 = bf16[32,6,96]{2,1,0:T(8,128)(2,1)S(1)} all-gather(bf16[1,6,96]{2,1,0:T(8,128)(2,1)} %bitcast.335), channel_id=3, replica_groups=mesh['dp'=8,'ffn'=4] {'dp','ffn'}, dimensions={0}, use_global_device_ids=true | all-gather | bytes 38016 | tf_op jit(solution)/shard_map/all_gather | solution.py:155
  148.4 70.6 %all-gather.2 = bf16[2048,128]{1,0:T(8,128)(2,1)S(1)} all-gather(bf16[64,128]{1,0:T(8,128)(2,1)} %param.22), channel_id=4, replica_groups=mesh['dp'=8,'ffn'=4] {'dp','ffn'}, dimensions={0}, use_global_device_ids=true | all-gather | bytes 540672 | tf_op jit(solution)/shard_map/all_gather | solution.py:152
  219.0 68.3 %all-gather.3 = bf16[2048,128]{1,0:T(8,128)(2,1)S(1)} all-gather(bf16[64,128]{1,0:T(8,128)(2,1)} %param.23), channel_id=5, replica_groups=mesh['dp'=8,'ffn'=4] {'dp','ffn'}, dimensions={0}, use_global_device_ids=true | all-gather | bytes 540672 | tf_op jit(solution)/shard_map/all_gather | solution.py:153
  296.0 6.0 copy.232
  302.0 6.7 reshape.581
  325.2 4.8 fusion.113
  355.1 59.9 %all-gather.23.cloned.1.call-done = bf16[2048,768]{1,0:T(8,128)(2,1)} async-done(((bf16[512,768]{1,0:T(8,128)(2,1)}), bf16[2048,768]{1,0:T(8,128)(2,1)}) %all-gather.23.cloned.1.call-update) | async-done | bytes 3145744 | tf_op jit(solution)/shard_map/all_gather | solution.py:258
  415.0 7.6 fusion.120
  422.5 56.6 %all-gather.17.cloned.1.call-done = bf16[2048,768]{1,0:T(8,128)(2,1)} async-done(((bf16[512,768]{1,0:T(8,128)(2,1)}), bf16[2048,768]{1,0:T(8,128)(2,1)}) %all-gather.17.cloned.1.call-update) | async-done | bytes 3145744 | tf_op jit(solution)/shard_map/all_gather | solution.py:258
  479.2 32.5 %fusion.6 = (bf16[2048,768]{1,0:T(8,128)(2,1)}, bf16[2048,768]{1,0:T(8,128)(2,1)}, f32[2048,768]{1,0:T(8,128)}) fusion(f32[768]{0:T(1024)S(1)} %convert_element_type.336, f32[2048,768]{1,0:T(8,128)} %fusion.120, bf16[2048,768]{1,0:T(8,128)(2,1)} %all-gather.17.cloned.1.call-done, bf16[768,768]{1,0:T(8,128)(2,1)} %all-gather.19.cloned.1.call-done), kind=kOutput, calls=%fused_computation.23 | convolution fusion | flops 2623537152 | bytes 23202816 | tf_op jit(solution)/shard_map/dot_general | solution.py:259
  511.7 7.5 fusion.119
  519.3 7.5 fusion.121
  527.7 101.1 %reduce-scatter.8.cloned.1.call-done = f32[512,768]{1,0:T(8,128)} async-done(((f32[2048,768]{1,0:T(8,128)}), f32[512,768]{1,0:T(8,128)}) %reduce-scatter.8.cloned.1.call-update) | async-done | bytes 1572880 | tf_op jit(solution)/shard_map/reduce_scatter | solution.py:264
  628.8 113.6 %reduce-scatter.10.cloned.1.call-done = f32[512,768]{1,0:T(8,128)} async-done(((f32[2048,768]{1,0:T(8,128)}), f32[512,768]{1,0:T(8,128)}) %reduce-scatter.10.cloned.1.call-update) | async-done | bytes 1572880 | tf_op jit(solution)/shard_map/reduce_scatter | solution.py:264
  756.4 61.5 %all-gather.25.cloned.1.call-done = bf16[2048,768]{1,0:T(8,128)(2,1)} async-done(((bf16[512,768]{1,0:T(8,128)(2,1)}), bf16[2048,768]{1,0:T(8,128)(2,1)}) %all-gather.25.cloned.1.call-update) | async-done | bytes 3145744 | tf_op jit(solution)/shard_map/all_gather | solution.py:272
  817.9 7.4 fusion.117
  827.0 4.6 fusion.122
  831.6 49.8 %all-gather.27.cloned.1.call-done = bf16[2048,768]{1,0:T(8,128)(2,1)} async-done(((bf16[512,768]{1,0:T(8,128)(2,1)}), bf16[2048,768]{1,0:T(8,128)(2,1)}) %all-gather.27.cloned.1.call-update) | async-done | bytes 3145744 | tf_op jit(solution)/shard_map/all_gather | solution.py:272
  881.5 7.4 fusion.118
  890.7 4.6 fusion.123
  897.4 95.8 %reduce-scatter.12.cloned.1.call-done = f32[512,768]{1,0:T(8,128)} async-done(((f32[2048,768]{1,0:T(8,128)}), f32[512,768]{1,0:T(8,128)}) %reduce-scatter.12.cloned.1.call-update) | async-done | bytes 1572880 | tf_op jit(solution)/shard_map/reduce_scatter | solution.py:279
  997.0 109.7 %reduce-scatter.14.cloned.1.call-done = f32[512,768]{1,0:T(8,128)} async-done(((f32[2048,768]{1,0:T(8,128)}), f32[512,768]{1,0:T(8,128)}) %reduce-scatter.14.cloned.1.call-update) | async-done | bytes 1572880 | tf_op jit(solution)/shard_map/reduce_scatter | solution.py:279
  1113.1 7.6 convert_reduce_fusion.8
  1120.7 8.9 multiply_reduce_fusion.1
  1132.0 7.6 convert_reduce_fusion.6
  1139.6 8.8 multiply_reduce_fusion
  1148.9 13.7 fusion.46
  1167.8 4.8 convert_reduce_fusion.9
  1172.6 13.6 fusion.48
  1211.4 5.0 multiply_convert_fusion.2
  1221.4 5.1 add_bitcast_fusion
  1226.5 8.0 copy.206
  1234.5 10.4 reshape.651
  1244.9 7.3 copy.207
  1265.8 6.6 convolution_convert_fusion
  1277.0 6.5 convolution_convert_fusion.2
  1283.5 10.3 all-to-all-done.5
  1298.1 6.6 convolution_convert_fusion.1
  1304.7 10.5 all-to-all-done.1
  1319.5 6.6 convolution_convert_fusion.3
  1326.1 10.4 all-to-all-done.4
  1349.2 8.9 all-to-all-done
  1360.5 39.7 %all-reduce = f32[32,2,96]{2,1,0:T(2,128)S(1)} all-reduce(f32[32,2,96]{2,1,0:T(2,128)S(1)} %bitcast.332), channel_id=19, replica_groups=mesh['dp'=8,'ffn'=4] {'dp','ffn'}, use_global_device_ids=true, to_apply=%region_40.41.clone | all-reduce | flops 6144 | bytes 49152
  1400.8 5.2 add_bitcast_fusion.2
  1411.2 48.5 %reduce-scatter.20.cloned.1.call-done = f32[1,64,128]{2,1,0:T(8,128)} async-done(((f32[32,64,128]{2,1,0:T(8,128)}), f32[1,64,128]{2,1,0:T(8,128)}) %reduce-scatter.20.cloned.1.call-update) | async-done | bytes 32784 | tf_op jit(solution)/shard_map/reduce_scatter | solution.py:192
  1459.7 104.6 %reduce-scatter.18.cloned.1.call-done = f32[1,96,192]{2,1,0:T(8,128)} async-done(((f32[32,96,192]{2,1,0:T(8,128)}), f32[1,96,192]{2,1,0:T(8,128)}) %reduce-scatter.18.cloned.1.call-update) | async-done | bytes 73744 | tf_op jit(solution)/shard_map/reduce_scatter | solution.py:189
  1564.2 128.5 %reduce-scatter.16.cloned.1.call-done = f32[1,96,576]{2,1,0:T(8,128)} async-done(((f32[32,96,576]{2,1,0:T(8,128)}), f32[1,96,576]{2,1,0:T(8,128)}) %reduce-scatter.16.cloned.1.call-update) | async-done | bytes 221200 | tf_op jit(solution)/shard_map/reduce_scatter | solution.py:186
  (304 shorter events, 172.5 us)
Async XLA Ops:
  7.2 284.6 %all-gather.31.cloned.1.call-start = ((), (), s32[]{:S(2)}) async-start(), calls=%async_computation.24 | async-start | bytes 1622016 | tf_op jit(solution)/shard_map/all_gather | solution.py:151
  7.9 288.0 %all-gather.29.cloned.1.call-start = ((), (), s32[]{:S(2)}) async-start(), calls=%async_computation.23 | async-start | bytes 4055040 | tf_op jit(solution)/shard_map/all_gather | solution.py:150
  8.7 346.4 %all-gather.19.cloned.1.call-start = ((), (), s32[]{:S(2)}) async-start(), calls=%async_computation.14 | async-start | bytes 1327104 | tf_op jit(solution)/shard_map/all_gather | solution.py:158
  9.4 405.6 %all-gather.23.cloned.1.call-start = ((), (), s32[]{:S(2)}) async-start(), calls=%async_computation.17 | async-start | bytes 3932160 | tf_op jit(solution)/shard_map/all_gather | solution.py:258
  316.5 21.9 %copy-start.4 = (bf16[512,768]{0,1:T(8,128)(2,1)}, bf16[512,768]{0,1:T(8,128)(2,1)S(1)}, u32[]{:S(2)}) copy-start(bf16[512,768]{0,1:T(8,128)(2,1)S(1)} %copy.196) | copy-start | bytes 2359300
  317.9 26.2 %copy-start.12 = (bf16[512,768]{0,1:T(8,128)(2,1)}, bf16[512,768]{0,1:T(8,128)(2,1)S(1)}, u32[]{:S(2)}) copy-start(bf16[512,768]{0,1:T(8,128)(2,1)S(1)} %copy.194) | copy-start | bytes 2359300
  322.6 7.4 copy-start.6
  325.2 6.7 copy-start.14
  330.0 4.7 copy-start.39
  331.8 6.6 copy-start.41
  344.1 5.4 copy-start.45
  353.8 125.4 %all-gather.17.cloned.1.call-start = ((), (), s32[]{:S(2)}) async-start(), calls=%async_computation.13 | async-start | bytes 3932160 | tf_op jit(solution)/shard_map/all_gather | solution.py:258
  354.4 157.3 %all-gather.21.cloned.1.call-start = ((), (), s32[]{:S(2)}) async-start(), calls=%async_computation.15 | async-start | bytes 1327104 | tf_op jit(solution)/shard_map/all_gather | solution.py:159
  355.0 273.8 %reduce-scatter.8.cloned.1.call-start = ((), (), s32[]{:S(2)}) async-start(), calls=%async_computation.16 | async-start | bytes 7864320 | tf_op jit(solution)/shard_map/reduce_scatter | solution.py:264
  519.2 223.2 %reduce-scatter.10.cloned.1.call-start = ((), (), s32[]{:S(2)}) async-start(), calls=%async_computation.18 | async-start | bytes 7864320 | tf_op jit(solution)/shard_map/reduce_scatter | solution.py:264
  526.8 291.1 %all-gather.25.cloned.1.call-start = ((), (), s32[]{:S(2)}) async-start(), calls=%async_computation.19 | async-start | bytes 3932160 | tf_op jit(solution)/shard_map/all_gather | solution.py:272
  753.7 127.8 %all-gather.27.cloned.1.call-start = ((), (), s32[]{:S(2)}) async-start(), calls=%async_computation.21 | async-start | bytes 3932160 | tf_op jit(solution)/shard_map/all_gather | solution.py:272
  756.3 236.9 %reduce-scatter.12.cloned.1.call-start = ((), (), s32[]{:S(2)}) async-start(), calls=%async_computation.20 | async-start | bytes 7864320 | tf_op jit(solution)/shard_map/reduce_scatter | solution.py:279
  817.9 9.1 copy-start.54
  831.6 275.1 %reduce-scatter.14.cloned.1.call-start = ((), (), s32[]{:S(2)}) async-start(), calls=%async_computation.22 | async-start | bytes 7864320 | tf_op jit(solution)/shard_map/reduce_scatter | solution.py:279
  881.5 9.2 copy-start.55
  895.3 514.6 %all-reduce.4.cloned.1.call-start = ((), (), s32[]{:S(2)}) async-start(), calls=%async_computation.28 | async-start | bytes 262144
  1106.7 5.3 copy-start.28
  1113.1 7.6 copy-start.15
  1120.7 8.9 copy-start.9
  1132.0 7.6 copy-start.13
  1162.6 5.2 copy-start.7
  1186.2 5.2 copy-start.5
  1196.2 263.5 %reduce-scatter.20.cloned.1.call-start = ((), (), s32[]{:S(2)}) async-start(), calls=%async_computation.27 | async-start | bytes 1081344 | tf_op jit(solution)/shard_map/reduce_scatter | solution.py:192
  1200.2 364.0 %reduce-scatter.18.cloned.1.call-start = ((), (), s32[]{:S(2)}) async-start(), calls=%async_computation.26 | async-start | bytes 3244032 | tf_op jit(solution)/shard_map/reduce_scatter | solution.py:189
  1210.3 482.4 %reduce-scatter.16.cloned.1.call-start = ((), (), s32[]{:S(2)}) async-start(), calls=%async_computation.25 | async-start | bytes 8110080 | tf_op jit(solution)/shard_map/reduce_scatter | solution.py:186
  1211.4 5.0 copy-start.25
  1211.4 5.0 copy-start.32
  1211.4 5.0 copy-start.38
  1211.4 7.0 slice-start
  1254.1 8.4 all-to-all-start.3
  1262.4 10.0 all-to-all-start.2
  1272.4 21.4 %all-to-all-start.5 = ((bf16[8,768,96]{1,2,0:T(8,128)(2,1)}), bf16[8,768,96]{1,2,0:T(8,128)(2,1)}, u32[]{:S(2)}, u32[]{:S(2)}) async-start(bf16[8,768,96]{1,2,0:T(8,128)(2,1)} %bitcast.320), calls=%async_computation.9 | async-start | bytes 2359296 | tf_op jit(solution)/shard_map/all_to_all | solution.py:22
  1293.8 21.3 %all-to-all-start.1 = ((bf16[8,96,768]{2,1,0:T(8,128)(2,1)}), bf16[8,96,768]{2,1,0:T(8,128)(2,1)}, u32[]{:S(2)}, u32[]{:S(2)}) async-start(bf16[8,96,768]{2,1,0:T(8,128)(2,1)} %bitcast.321), calls=%async_computation.5 | async-start | bytes 2359296 | tf_op jit(solution)/shard_map/all_to_all | solution.py:22
  1315.2 21.3 %all-to-all-start.4 = ((bf16[8,768,96]{1,2,0:T(8,128)(2,1)}), bf16[8,768,96]{1,2,0:T(8,128)(2,1)}, u32[]{:S(2)}, u32[]{:S(2)}) async-start(bf16[8,768,96]{1,2,0:T(8,128)(2,1)} %bitcast.322), calls=%async_computation.8 | async-start | bytes 2359296 | tf_op jit(solution)/shard_map/all_to_all | solution.py:22
  1319.4 21.3 %copy-start.51 = (f32[768]{0:T(1024)S(1)}, f32[768]{0:T(1024)}, u32[]{:S(2)}) copy-start(f32[768]{0:T(1024)} %get-tuple-element.16) | copy-start | bytes 9220
  1319.4 21.3 %copy-start.50 = (f32[768]{0:T(1024)S(1)}, f32[768]{0:T(1024)}, u32[]{:S(2)}) copy-start(f32[768]{0:T(1024)} %get-tuple-element.19) | copy-start | bytes 9220
  1319.5 21.4 %copy-start.16 = (bf16[1,512,768]{2,1,0:T(8,128)(2,1)S(1)}, bf16[1,512,768]{2,1,0:T(8,128)(2,1)}, u32[]{:S(2)}) copy-start(bf16[1,512,768]{2,1,0:T(8,128)(2,1)} %get-tuple-element.61) | copy-start | bytes 2359300
  1336.4 21.6 %all-to-all-start = ((bf16[8,96,768]{2,1,0:T(8,128)(2,1)}), bf16[8,96,768]{2,1,0:T(8,128)(2,1)}, u32[]{:S(2)}, u32[]{:S(2)}) async-start(bf16[8,96,768]{2,1,0:T(8,128)(2,1)} %bitcast.319), calls=%async_computation.4 | async-start | bytes 2359296 | tf_op jit(solution)/shard_map/all_to_all | solution.py:22
  1345.4 55.3 %copy-start.26 = (bf16[12,64,512]{2,1,0:T(8,128)(2,1)S(1)}, bf16[12,64,512]{2,1,0:T(8,128)(2,1)}, u32[]{:S(2)}) copy-start(bf16[12,64,512]{2,1,0:T(8,128)(2,1)} %get-tuple-element.98) | copy-start | bytes 2359300
  1400.8 5.2 copy-start.11
  1400.8 5.2 copy-start.18
  1400.8 5.2 copy-start.24
  (35 other events, 82.6 us)
Sparse Core Ops, SparseCore 0:
  10.9 57.7 all-gather.30
  71.5 60.2 all-gather.28
  133.7 22.7 all-gather.18
  353.9 61.0 all-gather.22
  417.0 62.1 all-gather.16
  480.9 22.7 all-gather.20
  519.4 109.3 reduce-scatter.7
  631.1 111.2 reduce-scatter.9
  753.8 64.0 all-gather.24
  819.3 62.1 all-gather.26
  883.8 109.3 reduce-scatter.11
  995.4 111.2 reduce-scatter.13
  1196.3 124.6 all-reduce.3
  1323.7 135.9 reduce-scatter.19
  1466.4 97.8 reduce-scatter.17
  1571.3 121.4 reduce-scatter.15
where the time goes:
time: 1710 us; the launch traced here: 1700 us
  waiting for transfers between devices  976 us (57%)
  blocking collectives  313 us (18%)
  matrix products  199 us (12%)
  local copies, waits for them, and re-layouts  92 us (5%)
  other arithmetic  78.4 us (5%)
  starting transfers between devices  25.4 us (1%)
    reduce_scatter x2, waiting for transfers between devices, micro_step(): lax.psum_scatter(partial_out, 'ffn', scatter_dimension=0, tiled=True)  215 us
    reduce_scatter x2, waiting for transfers between devices, micro_step(): lax.psum_scatter(grad_hidden_part, 'ffn', scatter_dimension=0, tiled=True)  206 us
    reduce_scatter x1, waiting for transfers between devices, reduce_grads(): lax.psum_scatter(disperse(grad_qkv, rows_dp, cols_ffn), ('dp', 'ffn'), sc...  129 us
    all_gather x2, waiting for transfers between devices, micro_step(): gathered = lax.all_gather(hidden_low, 'ffn', axis=0, tiled=True)  117 us
    all_gather x2, waiting for transfers between devices, micro_step(): grad_gathered = lax.all_gather(grad_second_low, 'ffn', axis=0, tiled=True)  111 us
    reduce_scatter x1, waiting for transfers between devices, reduce_grads(): lax.psum_scatter(disperse(grad_out, rows_dp, cols_ffn), ('dp', 'ffn'), sc...  105 us
    all_gather x1, blocking collectives, fetch_weights(): lax.all_gather(learned_gate_scores[None], ('dp', 'ffn'), axis=0, tiled=True)  70.6 us
    all_gather x1, blocking collectives, fetch_weights(): lax.all_gather(layernorm_scales[None], ('dp', 'ffn'), axis=0, tiled=True)  69.5 us
  transfers between devices with their start and end apart: 22, of which 16 were waited for; matrix products, arithmetic and copies ran while one was open for 15% of the time, Pallas kernels for 0%

commit v1 on v0

--- a/solution.py
+++ b/solution.py
@@ -146,11 +146,25 @@
 ):
     rows_dp = lax.axis_size("dp")
     cols_ffn = lax.axis_size("ffn")
+
+    def enter_the_indices(vals):
+        val2, tall = (jax.lax.axis_size(("dp", "ffn")), jax.lax.axis_index(("dp", "ffn")))
+        earlier, mixed_arr = (vals, 1)
+        while mixed_arr < val2:
+            block_now = jax.lax.ppermute(
+                earlier, ("dp", "ffn"), tuple(((dev_j, dev_j ^ mixed_arr) for dev_j in range(val2)))
+            )
+            d_next = jnp.concatenate([earlier, block_now], 0)
+            part_next = jnp.concatenate([block_now, earlier], axis=0)
+            earlier = jnp.where(tall & mixed_arr == 0, d_next, part_next)
+            mixed_arr = 2 * mixed_arr
+        return earlier
+
     tiles = (
         lax.all_gather(attention_triple_matrix[None], ("dp", "ffn"), axis=0, tiled=True),
         lax.all_gather(attention_final_matrix[None], ("dp", "ffn"), axis=0, tiled=True),
         lax.all_gather(learned_gate_scores[None], ("dp", "ffn"), axis=0, tiled=True),
-        lax.all_gather(fixed_jitter_matrix[None], ("dp", "ffn"), axis=0, tiled=True),
+        enter_the_indices(fixed_jitter_matrix[None]),
         lax.all_gather(layernorm_scales[None], ("dp", "ffn"), axis=0, tiled=True),
         lax.all_gather(offset_vectors[None], ("dp", "ffn"), axis=0, tiled=True),
     )

time: 1710 us -> 1650 us (0.965)
  blocking collectives: 313 us -> 241 us
    all_gather x1 -> x0, blocking collectives: 68.3 us -> none  [fetch_weights(): lax.all_gather(fixed_jitter_matrix[None], ('dp', 'ffn'), axis=0, tiled=True)]
  transfers between devices with their start and end apart: 22 -> 27, of which waited for: 16 -> 18; matrix products, arithmetic and copies ran while one was open for 15% -> 15% of each run, Pallas kernels for 0% -> 0%
where the time goes in v1:
time: 1650 us; the launch traced here: 1640 us
  waiting for transfers between devices  984 us (60%)
  blocking collectives  241 us (15%)
  matrix products  199 us (12%)
  local copies, waits for them, and re-layouts  92 us (6%)
  other arithmetic  79.4 us (5%)
  starting transfers between devices  30.1 us (2%)
    reduce_scatter x2, waiting for transfers between devices, micro_step(): lax.psum_scatter(partial_out, 'ffn', scatter_dimension=0, tiled=True)  215 us
    reduce_scatter x2, waiting for transfers between devices, micro_step(): lax.psum_scatter(grad_hidden_part, 'ffn', scatter_dimension=0, tiled=True)  206 us
    reduce_scatter x1, waiting for transfers between devices, reduce_grads(): lax.psum_scatter(disperse(grad_qkv, rows_dp, cols_ffn), ('dp', 'ffn'), sc...  128 us
    all_gather x2, waiting for transfers between devices, micro_step(): gathered = lax.all_gather(hidden_low, 'ffn', axis=0, tiled=True)  115 us
    all_gather x2, waiting for transfers between devices, micro_step(): grad_gathered = lax.all_gather(grad_second_low, 'ffn', axis=0, tiled=True)  111 us
    reduce_scatter x1, waiting for transfers between devices, reduce_grads(): lax.psum_scatter(disperse(grad_out, rows_dp, cols_ffn), ('dp', 'ffn'), sc...  105 us
    all_gather x1, blocking collectives, fetch_weights(): lax.all_gather(learned_gate_scores[None], ('dp', 'ffn'), axis=0, tiled=True)  69.9 us
    all_gather x1, blocking collectives, fetch_weights(): lax.all_gather(layernorm_scales[None], ('dp', 'ffn'), axis=0, tiled=True)  67.1 us
  transfers between devices with their start and end apart: 27, of which 18 were waited for; matrix products, arithmetic and copies ran while one was open for 15% of the time, Pallas kernels for 0%

profile of v1, /device:TPU:0, one launch (start us, length us, event | category | flops | bytes accessed | tf_op | source)
XLA Modules:
  0.0 1641.7 jit_solution(17114833822983341680)
XLA Ops:
  11.9 67.1 %all-gather.6 = bf16[32,2,96]{2,1,0:T(2,128)(2,1)S(1)} all-gather(bf16[1,2,96]{2,1,0:T(2,128)(2,1)} %bitcast.342), channel_id=6, replica_groups=mesh['dp'=8,'ffn'=4] {'dp','ffn'}, dimensions={0}, use_global_device_ids=true | all-gather | bytes 12672 | tf_op jit(solution)/shard_map/all_gather | solution.py:168
  78.9 64.7 %all-gather.5 = bf16[32,6,96]{2,1,0:T(8,128)(2,1)S(1)} all-gather(bf16[1,6,96]{2,1,0:T(8,128)(2,1)} %bitcast.341), channel_id=3, replica_groups=mesh['dp'=8,'ffn'=4] {'dp','ffn'}, dimensions={0}, use_global_device_ids=true | all-gather | bytes 38016 | tf_op jit(solution)/shard_map/all_gather | solution.py:169
  152.2 5.4 collective-permute-done.3
  161.3 69.9 %all-gather.2 = bf16[2048,128]{1,0:T(8,128)(2,1)S(1)} all-gather(bf16[64,128]{1,0:T(8,128)(2,1)} %param.22), channel_id=4, replica_groups=mesh['dp'=8,'ffn'=4] {'dp','ffn'}, dimensions={0}, use_global_device_ids=true | all-gather | bytes 540672 | tf_op jit(solution)/shard_map/all_gather | solution.py:166
  239.3 6.0 copy.232
  245.4 6.7 reshape.585
  268.5 4.8 fusion.114
  298.4 58.4 %all-gather.22.cloned.1.call-done = bf16[2048,768]{1,0:T(8,128)(2,1)} async-done(((bf16[512,768]{1,0:T(8,128)(2,1)}), bf16[2048,768]{1,0:T(8,128)(2,1)}) %all-gather.22.cloned.1.call-update) | async-done | bytes 3145744 | tf_op jit(solution)/shard_map/all_gather | solution.py:272
  356.9 7.6 fusion.121
  364.4 56.6 %all-gather.16.cloned.1.call-done = bf16[2048,768]{1,0:T(8,128)(2,1)} async-done(((bf16[512,768]{1,0:T(8,128)(2,1)}), bf16[2048,768]{1,0:T(8,128)(2,1)}) %all-gather.16.cloned.1.call-update) | async-done | bytes 3145744 | tf_op jit(solution)/shard_map/all_gather | solution.py:272
  421.1 32.5 %fusion.6 = (bf16[2048,768]{1,0:T(8,128)(2,1)}, bf16[2048,768]{1,0:T(8,128)(2,1)}, f32[2048,768]{1,0:T(8,128)}) fusion(f32[768]{0:T(1024)S(1)} %convert_element_type.336, f32[2048,768]{1,0:T(8,128)} %fusion.121, bf16[2048,768]{1,0:T(8,128)(2,1)} %all-gather.16.cloned.1.call-done, bf16[768,768]{1,0:T(8,128)(2,1)} %all-gather.18.cloned.1.call-done), kind=kOutput, calls=%fused_computation.23 | convolution fusion | flops 2623537152 | bytes 23202816 | tf_op jit(solution)/shard_map/dot_general | solution.py:273
  453.6 7.5 fusion.120
  461.2 7.5 fusion.122
  469.6 101.1 %reduce-scatter.8.cloned.1.call-done = f32[512,768]{1,0:T(8,128)} async-done(((f32[2048,768]{1,0:T(8,128)}), f32[512,768]{1,0:T(8,128)}) %reduce-scatter.8.cloned.1.call-update) | async-done | bytes 1572880 | tf_op jit(solution)/shard_map/reduce_scatter | solution.py:278
  570.7 113.6 %reduce-scatter.10.cloned.1.call-done = f32[512,768]{1,0:T(8,128)} async-done(((f32[2048,768]{1,0:T(8,128)}), f32[512,768]{1,0:T(8,128)}) %reduce-scatter.10.cloned.1.call-update) | async-done | bytes 1572880 | tf_op jit(solution)/shard_map/reduce_scatter | solution.py:278
  698.3 61.5 %all-gather.24.cloned.1.call-done = bf16[2048,768]{1,0:T(8,128)(2,1)} async-done(((bf16[512,768]{1,0:T(8,128)(2,1)}), bf16[2048,768]{1,0:T(8,128)(2,1)}) %all-gather.24.cloned.1.call-update) | async-done | bytes 3145744 | tf_op jit(solution)/shard_map/all_gather | solution.py:286
  759.8 7.5 fusion.118
  768.9 4.6 fusion.123
  773.5 49.8 %all-gather.26.cloned.1.call-done = bf16[2048,768]{1,0:T(8,128)(2,1)} async-done(((bf16[512,768]{1,0:T(8,128)(2,1)}), bf16[2048,768]{1,0:T(8,128)(2,1)}) %all-gather.26.cloned.1.call-update) | async-done | bytes 3145744 | tf_op jit(solution)/shard_map/all_gather | solution.py:286
  823.4 7.4 fusion.119
  832.6 4.6 fusion.124
  839.3 95.8 %reduce-scatter.12.cloned.1.call-done = f32[512,768]{1,0:T(8,128)} async-done(((f32[2048,768]{1,0:T(8,128)}), f32[512,768]{1,0:T(8,128)}) %reduce-scatter.12.cloned.1.call-update) | async-done | bytes 1572880 | tf_op jit(solution)/shard_map/reduce_scatter | solution.py:293
  938.8 109.7 %reduce-scatter.14.cloned.1.call-done = f32[512,768]{1,0:T(8,128)} async-done(((f32[2048,768]{1,0:T(8,128)}), f32[512,768]{1,0:T(8,128)}) %reduce-scatter.14.cloned.1.call-update) | async-done | bytes 1572880 | tf_op jit(solution)/shard_map/reduce_scatter | solution.py:293
  1055.0 7.6 convert_reduce_fusion.8
  1062.6 8.9 multiply_reduce_fusion.1
  1073.9 7.6 convert_reduce_fusion.6
  1081.5 8.8 multiply_reduce_fusion
  1090.8 13.7 fusion.46
  1109.6 4.8 convert_reduce_fusion.9
  1114.5 13.6 fusion.48
  1153.3 5.0 multiply_convert_fusion.2
  1163.3 5.1 add_bitcast_fusion
  1168.4 8.0 copy.206
  1176.4 10.4 reshape.648
  1186.8 7.3 copy.207
  1207.7 6.6 convolution_convert_fusion
  1218.8 6.5 convolution_convert_fusion.2
  1225.4 10.3 all-to-all-done.5
  1240.0 6.6 convolution_convert_fusion.1
  1246.6 10.5 all-to-all-done.1
  1261.3 6.6 convolution_convert_fusion.3
  1267.9 10.4 all-to-all-done.4
  1291.1 8.9 all-to-all-done
  1302.3 39.8 %all-reduce = f32[32,2,96]{2,1,0:T(2,128)S(1)} all-reduce(f32[32,2,96]{2,1,0:T(2,128)S(1)} %bitcast.336), channel_id=18, replica_groups=mesh['dp'=8,'ffn'=4] {'dp','ffn'}, use_global_device_ids=true, to_apply=%region_40.41.clone | all-reduce | flops 6144 | bytes 49152
  1342.7 5.2 add_bitcast_fusion.2
  1353.1 48.3 %reduce-scatter.20.cloned.1.call-done = f32[1,64,128]{2,1,0:T(8,128)} async-done(((f32[32,64,128]{2,1,0:T(8,128)}), f32[1,64,128]{2,1,0:T(8,128)}) %reduce-scatter.20.cloned.1.call-update) | async-done | bytes 32784 | tf_op jit(solution)/shard_map/reduce_scatter | solution.py:206
  1401.4 104.9 %reduce-scatter.18.cloned.1.call-done = f32[1,96,192]{2,1,0:T(8,128)} async-done(((f32[32,96,192]{2,1,0:T(8,128)}), f32[1,96,192]{2,1,0:T(8,128)}) %reduce-scatter.18.cloned.1.call-update) | async-done | bytes 73744 | tf_op jit(solution)/shard_map/reduce_scatter | solution.py:203
  1506.3 128.4 %reduce-scatter.16.cloned.1.call-done = f32[1,96,576]{2,1,0:T(8,128)} async-done(((f32[32,96,576]{2,1,0:T(8,128)}), f32[1,96,576]{2,1,0:T(8,128)}) %reduce-scatter.16.cloned.1.call-update) | async-done | bytes 221200 | tf_op jit(solution)/shard_map/reduce_scatter | solution.py:200
  (317 shorter events, 181.7 us)
Async XLA Ops:
  7.2 228.0 %all-gather.30.cloned.1.call-start = ((), (), s32[]{:S(2)}) async-start(), calls=%async_computation.24 | async-start | bytes 1622016 | tf_op jit(solution)/shard_map/all_gather | solution.py:165
  7.9 231.4 %all-gather.28.cloned.1.call-start = ((), (), s32[]{:S(2)}) async-start(), calls=%async_computation.23 | async-start | bytes 4055040 | tf_op jit(solution)/shard_map/all_gather | solution.py:164
  8.7 289.8 %all-gather.18.cloned.1.call-start = ((), (), s32[]{:S(2)}) async-start(), calls=%async_computation.14 | async-start | bytes 1327104 | tf_op jit(solution)/shard_map/all_gather | solution.py:172
  8.7 134.9 %collective-permute-start = (bf16[1,64,128]{2,1,0:T(8,128)(2,1)}, bf16[1,64,128]{2,1,0:T(8,128)(2,1)S(1)}, u32[]{:S(2)}, u32[]{:S(2)}) collective-permute-start(bf16[1,64,128]{2,1,0:T(8,128)(2,1)} %bitcast.339), channel_id=1, source_target_pairs={{0,1},{1,0},{2,3},{3,2},{4,5},{5,4},{6,7},{7,6},{8,9},{9,8},{10,11... | collective-permute-start | bytes 49160 | tf_op jit(solution)/shard_map/ppermute | solution.py:154
  11.8 345.1 %all-gather.22.cloned.1.call-start = ((), (), s32[]{:S(2)}) async-start(), calls=%async_computation.17 | async-start | bytes 3932160 | tf_op jit(solution)/shard_map/all_gather | solution.py:272
  144.5 4.8 collective-permute-start.1
  149.3 1.4 collective-permute-start.2
  150.7 6.9 collective-permute-start.3
  157.7 73.5 %collective-permute-start.4 = (bf16[16,64,128]{2,1,0:T(8,128)(2,1)S(1)}, bf16[16,64,128]{2,1,0:T(8,128)(2,1)S(1)}, u32[]{:S(2)}, u32[]{:S(2)}) collective-permute-start(bf16[16,64,128]{2,1,0:T(8,128)(2,1)S(1)} %maximum_select_fusion.1), channel_id=1, source_target_pairs={{0,16},{1,17},{2,18},{3,19},{4,20},{5,21},{6,22},{7,23},{8,24},{9,... | collective-permute-start | bytes 786440 | tf_op jit(solution)/shard_map/ppermute | solution.py:154
  259.8 21.9 %copy-start.4 = (bf16[512,768]{0,1:T(8,128)(2,1)}, bf16[512,768]{0,1:T(8,128)(2,1)S(1)}, u32[]{:S(2)}) copy-start(bf16[512,768]{0,1:T(8,128)(2,1)S(1)} %copy.196) | copy-start | bytes 2359300
  261.3 26.2 %copy-start.12 = (bf16[512,768]{0,1:T(8,128)(2,1)}, bf16[512,768]{0,1:T(8,128)(2,1)S(1)}, u32[]{:S(2)}) copy-start(bf16[512,768]{0,1:T(8,128)(2,1)S(1)} %copy.194) | copy-start | bytes 2359300
  265.9 7.4 copy-start.6
  268.5 6.7 copy-start.14
  275.2 6.6 copy-start.41
  287.5 5.4 copy-start.45
  297.2 123.9 %all-gather.16.cloned.1.call-start = ((), (), s32[]{:S(2)}) async-start(), calls=%async_computation.13 | async-start | bytes 3932160 | tf_op jit(solution)/shard_map/all_gather | solution.py:272
  297.8 155.8 %all-gather.20.cloned.1.call-start = ((), (), s32[]{:S(2)}) async-start(), calls=%async_computation.15 | async-start | bytes 1327104 | tf_op jit(solution)/shard_map/all_gather | solution.py:173
  298.3 272.3 %reduce-scatter.8.cloned.1.call-start = ((), (), s32[]{:S(2)}) async-start(), calls=%async_computation.16 | async-start | bytes 7864320 | tf_op jit(solution)/shard_map/reduce_scatter | solution.py:278
  461.1 223.2 %reduce-scatter.10.cloned.1.call-start = ((), (), s32[]{:S(2)}) async-start(), calls=%async_computation.18 | async-start | bytes 7864320 | tf_op jit(solution)/shard_map/reduce_scatter | solution.py:278
  468.7 291.1 %all-gather.24.cloned.1.call-start = ((), (), s32[]{:S(2)}) async-start(), calls=%async_computation.19 | async-start | bytes 3932160 | tf_op jit(solution)/shard_map/all_gather | solution.py:286
  695.6 127.8 %all-gather.26.cloned.1.call-start = ((), (), s32[]{:S(2)}) async-start(), calls=%async_computation.21 | async-start | bytes 3932160 | tf_op jit(solution)/shard_map/all_gather | solution.py:286
  698.2 236.9 %reduce-scatter.12.cloned.1.call-start = ((), (), s32[]{:S(2)}) async-start(), calls=%async_computation.20 | async-start | bytes 7864320 | tf_op jit(solution)/shard_map/reduce_scatter | solution.py:293
  759.8 9.1 copy-start.54
  773.5 275.1 %reduce-scatter.14.cloned.1.call-start = ((), (), s32[]{:S(2)}) async-start(), calls=%async_computation.22 | async-start | bytes 7864320 | tf_op jit(solution)/shard_map/reduce_scatter | solution.py:293
  823.4 9.2 copy-start.55
  837.2 514.6 %all-reduce.4.cloned.1.call-start = ((), (), s32[]{:S(2)}) async-start(), calls=%async_computation.28 | async-start | bytes 262144
  1048.6 5.3 copy-start.28
  1055.0 7.6 copy-start.15
  1062.6 8.9 copy-start.9
  1073.9 7.6 copy-start.13
  1104.5 5.2 copy-start.7
  1138.1 263.3 %reduce-scatter.20.cloned.1.call-start = ((), (), s32[]{:S(2)}) async-start(), calls=%async_computation.27 | async-start | bytes 1081344 | tf_op jit(solution)/shard_map/reduce_scatter | solution.py:206
  1142.1 364.2 %reduce-scatter.18.cloned.1.call-start = ((), (), s32[]{:S(2)}) async-start(), calls=%async_computation.26 | async-start | bytes 3244032 | tf_op jit(solution)/shard_map/reduce_scatter | solution.py:203
  1152.2 482.5 %reduce-scatter.16.cloned.1.call-start = ((), (), s32[]{:S(2)}) async-start(), calls=%async_computation.25 | async-start | bytes 8110080 | tf_op jit(solution)/shard_map/reduce_scatter | solution.py:200
  1153.3 7.0 slice-start
  1196.0 8.4 all-to-all-start.3
  1204.3 10.0 all-to-all-start.2
  1214.3 21.4 %all-to-all-start.5 = ((bf16[8,768,96]{1,2,0:T(8,128)(2,1)}), bf16[8,768,96]{1,2,0:T(8,128)(2,1)}, u32[]{:S(2)}, u32[]{:S(2)}) async-start(bf16[8,768,96]{1,2,0:T(8,128)(2,1)} %bitcast.324), calls=%async_computation.9 | async-start | bytes 2359296 | tf_op jit(solution)/shard_map/all_to_all | solution.py:22
  1235.7 21.3 %all-to-all-start.1 = ((bf16[8,96,768]{2,1,0:T(8,128)(2,1)}), bf16[8,96,768]{2,1,0:T(8,128)(2,1)}, u32[]{:S(2)}, u32[]{:S(2)}) async-start(bf16[8,96,768]{2,1,0:T(8,128)(2,1)} %bitcast.325), calls=%async_computation.5 | async-start | bytes 2359296 | tf_op jit(solution)/shard_map/all_to_all | solution.py:22
  1257.1 21.3 %all-to-all-start.4 = ((bf16[8,768,96]{1,2,0:T(8,128)(2,1)}), bf16[8,768,96]{1,2,0:T(8,128)(2,1)}, u32[]{:S(2)}, u32[]{:S(2)}) async-start(bf16[8,768,96]{1,2,0:T(8,128)(2,1)} %bitcast.326), calls=%async_computation.8 | async-start | bytes 2359296 | tf_op jit(solution)/shard_map/all_to_all | solution.py:22
  1261.3 21.3 %copy-start.51 = (f32[768]{0:T(1024)S(1)}, f32[768]{0:T(1024)}, u32[]{:S(2)}) copy-start(f32[768]{0:T(1024)} %get-tuple-element.16) | copy-start | bytes 9220
  1261.3 21.3 %copy-start.50 = (f32[768]{0:T(1024)S(1)}, f32[768]{0:T(1024)}, u32[]{:S(2)}) copy-start(f32[768]{0:T(1024)} %get-tuple-element.19) | copy-start | bytes 9220
  1261.3 21.4 %copy-start.16 = (bf16[1,512,768]{2,1,0:T(8,128)(2,1)S(1)}, bf16[1,512,768]{2,1,0:T(8,128)(2,1)}, u32[]{:S(2)}) copy-start(bf16[1,512,768]{2,1,0:T(8,128)(2,1)} %get-tuple-element.61) | copy-start | bytes 2359300
  1278.3 21.6 %all-to-all-start = ((bf16[8,96,768]{2,1,0:T(8,128)(2,1)}), bf16[8,96,768]{2,1,0:T(8,128)(2,1)}, u32[]{:S(2)}, u32[]{:S(2)}) async-start(bf16[8,96,768]{2,1,0:T(8,128)(2,1)} %bitcast.323), calls=%async_computation.4 | async-start | bytes 2359296 | tf_op jit(solution)/shard_map/all_to_all | solution.py:22
  1287.3 55.4 %copy-start.26 = (bf16[12,64,512]{2,1,0:T(8,128)(2,1)S(1)}, bf16[12,64,512]{2,1,0:T(8,128)(2,1)}, u32[]{:S(2)}) copy-start(bf16[12,64,512]{2,1,0:T(8,128)(2,1)} %get-tuple-element.98) | copy-start | bytes 2359300
  1342.7 5.2 copy-start.11
  1342.7 5.2 copy-start.18
  1342.7 5.2 copy-start.24
  (40 other events, 107.1 us)
Sparse Core Ops, SparseCore 0:
  10.9 57.7 all-gather.29
  71.5 60.1 all-gather.27
  133.6 23.7 all-gather.17
  297.3 59.5 all-gather.21
  358.9 62.1 all-gather.15
  422.8 22.7 all-gather.19
  461.2 109.3 reduce-scatter.7
  573.0 111.2 reduce-scatter.9
  695.7 64.0 all-gather.23
  761.2 62.1 all-gather.25
  825.7 109.3 reduce-scatter.11
  937.2 111.2 reduce-scatter.13
  1138.2 124.6 all-reduce.3
  1265.6 135.7 reduce-scatter.19
  1408.1 98.1 reduce-scatter.17
  1513.4 121.2 reduce-scatter.15
